TPU v7x, 32 devices: a whole 2x2x4 slice. The times are simulated.
32 devices in a mesh: ctx: 8 (over y, x, core), mp: 4 (over z).
Axes of the slice: x: 2, y: 2, z: 4, core: 2. Of those that a mesh axis runs over, the one named last changes fastest.
Arguments:
- resid_in: bfloat16 [4096, 8192], P('ctx', 'mp'), may hold values from -6 to 6
- q_mr: bfloat16 [4096, 8192], P('ctx', 'mp'), may hold values from -6 to 6
- k_mr: bfloat16 [4096, 8192], P('ctx', 'mp'), may hold values from -6 to 6
- v_mr: bfloat16 [4096, 8192], P('ctx', 'mp'), may hold values from -6 to 6
- mr_filter: float32 [128, 8192], P(None, 'mp'), may hold values from -0.5 to 0.5
- mr_out: bfloat16 [8192, 8192], P('ctx', 'mp'), may hold values from -0.0625 to 0.0625
- q_li: bfloat16 [4096, 8192], P('ctx', 'mp'), may hold values from -6 to 6
- k_li: bfloat16 [4096, 8192], P('ctx', 'mp'), may hold values from -6 to 6
- li_rate: float32 [8192], P('mp'), may hold values from 2.4414063e-05 to 0.0333333333
- li_residue: float32 [8192], P('mp'), may hold values from 0.5 to 2
Outputs:
- mixed: bfloat16 [4096, 8192], P('ctx', 'mp')
- long_out: bfloat16 [4096, 8192], P('ctx', 'mp')
All inputs are finite; a program needn't handle non-finite values.
Results may differ from a plain program's by a relative error of at most 0.008.
Values may be sent and summed in bfloat16 or wider, within the bound.
A program may use at most 192 MiB of HBM per device.

v0:
```python
import jax
import jax.numpy as jnp
from jax import lax
from jax.sharding import PartitionSpec as P


def passed_along(value, axis, by):
    peers = lax.axis_size(axis)
    pairs = [(i, i + by) for i in range(peers) if 0 <= i + by < peers]
    return lax.ppermute(value, axis, pairs)


def carried_in(value, axis, join, neutral):
    count, mine = (lax.axis_size(axis), lax.axis_index(axis))
    pieces = jax.tree.map(lambda part: lax.all_gather(part, axis), value)
    subtotal = jax.tree.map(
        lambda part, zero: jnp.full_like(part, 0) + jnp.asarray(zero, part.dtype), value, neutral
    )

    def step(position, subtotal):
        longer = join(subtotal, jax.tree.map(lambda part: part[position], pieces))
        return jax.tree.map(lambda new, old: jnp.where(position < mine, new, old), longer, subtotal)

    return lax.fori_loop(0, count - 1, step, subtotal)


def link_pair(earlier, later):
    return (earlier[0] * later[0], later[0] * earlier[1] + later[1])


def body(resid_in, q_mr, k_mr, v_mr, mr_filter, mr_out, q_li, k_li, li_rate, li_residue):
    row_count = q_mr.shape[0]
    chan_count = q_mr.shape[1]
    tap_count = mr_filter.shape[0]
    drive_mr = (k_mr.astype(jnp.float32) * v_mr.astype(jnp.float32)).astype(jnp.bfloat16)
    prev_rows = passed_along(drive_mr[row_count - (tap_count - 1) :], "ctx", 1)
    padded = jnp.concatenate([prev_rows, drive_mr], 0).astype(jnp.float32)[None]
    kernel = mr_filter[::-1][:, None, :]
    filtered = lax.conv_general_dilated(
        padded,
        kernel,
        (1,),
        "VALID",
        dimension_numbers=("NWC", "WIO", "NWC"),
        feature_group_count=chan_count,
        precision=lax.Precision.HIGHEST,
    )[0]
    gated = (q_mr.astype(jnp.float32) * filtered).astype(jnp.bfloat16)
    gathered = lax.all_gather(gated, "mp", axis=1, tiled=True)
    all_rows = lax.all_gather(mr_out, "ctx", axis=0, tiled=True)
    summed = jnp.dot(gathered, all_rows, preferred_element_type=jnp.float32)
    mixed = (resid_in.astype(jnp.float32) + summed).astype(jnp.bfloat16)
    decay = jnp.exp(-li_rate)
    drive_li = k_li.astype(jnp.float32) * mixed.astype(jnp.float32)
    decay_rows = jnp.broadcast_to(decay[None, :], drive_li.shape)
    _, local_state = lax.associative_scan(link_pair, (decay_rows, drive_li), axis=0)
    offsets = jnp.arange(1, row_count + 1, dtype=jnp.float32)[:, None]
    powers = jnp.exp(-li_rate[None, :] * offsets)
    block_end = local_state[row_count - 1]
    block_decay = jnp.exp(-li_rate * row_count)
    identity = (jnp.ones_like(block_decay), jnp.zeros_like(block_end))
    prefix = carried_in((block_decay, block_end), "ctx", link_pair, identity)
    carried = prefix[1]
    state = local_state + powers * carried[None, :]
    scale = li_residue * jnp.sqrt(-jnp.expm1(-2.0 * li_rate))
    long_out = (q_li.astype(jnp.float32) * scale * state).astype(jnp.bfloat16)
    return (mixed, long_out)


def solution(mesh):
    in_specs = (
        P("ctx", "mp"),
        P("ctx", "mp"),
        P("ctx", "mp"),
        P("ctx", "mp"),
        P(None, "mp"),
        P("ctx", "mp"),
        P("ctx", "mp"),
        P("ctx", "mp"),
        P("mp"),
        P("mp"),
    )
    out_specs = (P("ctx", "mp"), P("ctx", "mp"))
    return jax.shard_map(body, mesh=mesh, in_specs=in_specs, out_specs=out_specs, check_vma=False)
```

profile of v0, /device:TPU:0, one launch (start us, length us, event | category | flops | bytes accessed | tf_op | source)
XLA Modules:
  0.0 563.9 jit_solution(2799196935869276048)
XLA Ops:
  7.2 3.1 multiply_convert_fusion.1
  11.2 3.2 collective-permute-start
  14.4 5.2 rev.3
  21.4 45.6 %fusion = f32[1,512,2048]{2,0,1:T(1,128)S(1)} fusion(bf16[1,639,2048]{2,1,0:T(8,128)(2,1)S(1)} %maximum_bitcast_fusion, f32[128,1,2048]{2,0,1:T(8,128)S(1)} %bitcast.22), kind=kOutput, calls=%fused_computation.3 | convolution fusion | flops 1610612736 | bytes 7860224 | tf_op jit(solution)/shard_map/conv_general_dilated | solution.py:39
  67.0 2.9 fusion.2
  71.4 14.1 %all-gather = f32[16384]{0:T(1024)S(1)} all-gather(f32[2048]{0:T(1024)S(1)} %get-tuple-element.139), channel_id=2, replica_groups=mesh['ctx'=8,'mp'=4] {'ctx'}, dimensions={0}, use_global_device_ids=true | all-gather | bytes 73728 | tf_op jit(solution)/shard_map/all_gather | solution.py:15
  86.8 138.0 %all-gather.5.cloned.1.call-done = bf16[512,8192]{1,0:T(8,128)(2,1)} async-done(((bf16[512,2048]{1,0:T(8,128)(2,1)}), bf16[512,8192]{1,0:T(8,128)(2,1)}) %all-gather.5.cloned.1.call-update) | async-done | bytes 8388624 | tf_op jit(solution)/shard_map/all_gather | solution.py:49
  224.8 160.9 %all-gather.7.cloned.1.call-done = bf16[8192,2048]{1,0:T(8,128)(2,1)} async-done(((bf16[1024,2048]{1,0:T(8,128)(2,1)}), bf16[8192,2048]{1,0:T(8,128)(2,1)}) %all-gather.7.cloned.1.call-update) | async-done | bytes 33554448 | tf_op jit(solution)/shard_map/all_gather | solution.py:50
  385.6 25.6 %convert_multiply_fusion = (f32[512,2048]{1,0:T(8,128)}, bf16[512,2048]{1,0:T(8,128)(2,1)}) fusion(bf16[512,2048]{1,0:T(8,128)(2,1)} %param.19, bf16[512,8192]{1,0:T(8,128)(2,1)} %all-gather.5.cloned.1.call-done, bf16[8192,2048]{1,0:T(8,128)(2,1)} %all-gather.7.cloned.1.call-done, bf16[512,2048]{1,0:T(8,128)(2,1)} %param.12), kind=kOutput, calls=%fused_computation.8 | convolution fusion | flops 17186160640 | bytes 52428800 | tf_op jit(solution)/shard_map/dot_general | solution.py:51
  411.3 10.0 %slice.254 = f32[255,2048]{1,0:T(8,128)} slice(f32[512,2048]{1,0:T(8,128)} %get-tuple-element.143), slice={[2:512:2], [0:2048:1]} | slice | bytes 4177920 | tf_op jit(solution)/shard_map/slice | solution.py:56
  421.3 9.8 %slice.200 = f32[256,2048]{1,0:T(8,128)} slice(f32[512,2048]{1,0:T(8,128)} %get-tuple-element.143), slice={[1:512:2], [0:2048:1]} | slice | bytes 4194304 | tf_op jit(solution)/shard_map/slice | solution.py:56
  431.1 9.8 %slice.199 = f32[256,2048]{1,0:T(8,128)} slice(f32[512,2048]{1,0:T(8,128)} %get-tuple-element.143), slice={[0:511:2], [0:2048:1]} | slice | bytes 4194304 | tf_op jit(solution)/shard_map/slice | solution.py:56
  440.9 2.6 multiply_add_fusion
  443.5 2.9 slice.205
  446.4 2.8 slice.204
  479.6 3.0 slice.252
  491.3 4.2 pad.70
  497.4 4.9 pad.69
  502.3 3.4 add.183
  507.9 16.7 %pad.71 = f32[512,2048]{1,0:T(8,128)} pad(f32[256,2048]{1,0:T(8,128)} %pad_maximum_fusion, f32[]{:T(128)} %constant.35.clone.1), padding=0_1_1x0_0_0 | pad | bytes 6291460 | tf_op jit(solution)/shard_map/pad | solution.py:56
  524.7 9.1 %pad.72 = f32[512,2048]{1,0:T(8,128)} pad(f32[256,2048]{1,0:T(8,128)S(1)} %copy-done.3, f32[]{:T(128)} %constant.35.clone.1), padding=1_0_1x0_0_0 | pad | bytes 6291460 | tf_op jit(solution)/shard_map/pad | solution.py:56
  534.6 9.2 %all-gather.1 = f32[8,1,2048]{2,1,0:T(1,128)S(1)} all-gather(f32[1,1,2048]{2,1,0:T(1,128)S(1)} %add_bitcast_fusion), channel_id=1, replica_groups=mesh['ctx'=8,'mp'=4] {'ctx'}, dimensions={0}, use_global_device_ids=true | all-gather | bytes 73728 | tf_op jit(solution)/shard_map/all_gather | solution.py:15
  543.8 6.3 %while.14 = (s32[]{:T(128)}, f32[2048]{0:T(1024)S(1)}, s32[]{:T(128)}, f32[8,2048]{1,0:T(8,128)}, f32[8,2048]{1,0:T(8,128)S(1)}, /*index=5*/s32[]{:T(128)}, s32[]{:T(128)}) while((s32[]{:T(128)}, f32[2048]{0:T(1024)S(1)}, s32[]{:T(128)}, f32[8,2048]{1,0:T(8,128)}, f32[8,2048]{1,0:T(8,128)S(1)}, /*index=5*/s32[]{:T(128)}, ...), condition=%wide.region_1.2_spmd.clone, body=%wide.region_0.1_spmd.clone.sunk | while | flops 8196 | bytes 65645 | solution.py:24
  550.2 6.9 %multiply_convert_fusion = bf16[512,2048]{1,0:T(8,128)(2,1)} fusion(f32[512,2048]{1,0:T(8,128)} %pad.71, f32[512,2048]{1,0:T(8,128)} %pad.72, bf16[512,2048]{1,0:T(8,128)(2,1)} %param.18, f32[2048]{0:T(1024)S(1)} %get-tuple-element.96, f32[512]{0:T(512)S(1)} %copy-done.28, f32[2048]{0:T(1024)S(1)} %copy-done.24, f32[2048]{0:T(1024)S(1)} %copy-done.23), kind=kLoop, calls=%fused_computation.7 | loop fusion | flops 8388608 | bytes 12609536 | tf_op jit(solution)/shard_map/convert_element_type | solution.py:66
  (160 shorter events, 55.2 us)
Async XLA Ops:
  7.2 7.2 %copy-start.8 = (f32[128,2048]{1,0:T(8,128)S(1)}, f32[128,2048]{1,0:T(8,128)}, u32[]{:S(2)}) copy-start(f32[128,2048]{1,0:T(8,128)} %param.16) | copy-start | bytes 3145732
  7.2 217.6 %all-gather.5.cloned.1.call-start = ((), (), s32[]{:S(2)}) async-start(), calls=%async_computation | async-start | bytes 10485760 | tf_op jit(solution)/shard_map/all_gather | solution.py:49
  11.2 8.3 %collective-permute-start = (bf16[127,2048]{1,0:T(8,128)(2,1)}, bf16[127,2048]{1,0:T(8,128)(2,1)}, u32[]{:S(2)}, u32[]{:S(2)}) collective-permute-start(bf16[127,2048]{1,0:T(8,128)(2,1)} %slice.256), channel_id=1, source_target_pairs={{0,4},{4,8},{8,12},{12,16},{16,20},{20,24},{24,28},{1,5},{5,9},{9,... | collective-permute-start | bytes 1560584 | tf_op jit(solution)/shard_map/ppermute | solution.py:10
  21.4 45.6 %copy-start.7 = (bf16[512,2048]{1,0:T(8,128)(2,1)S(1)}, bf16[512,2048]{1,0:T(8,128)(2,1)}, u32[]{:S(2)}) copy-start(bf16[512,2048]{1,0:T(8,128)(2,1)} %param.13) | copy-start | bytes 6291460
  69.9 315.7 %all-gather.7.cloned.1.call-start = ((), (), s32[]{:S(2)}) async-start(), calls=%async_computation.1 | async-start | bytes 37748736 | tf_op jit(solution)/shard_map/all_gather | solution.py:50
  71.3 369.6 %copy-start.12 = (f32[2048]{0:T(1024)}, f32[2048]{0:T(1024)S(1)}, u32[]{:S(2)}) copy-start(f32[2048]{0:T(1024)S(1)} %get-tuple-element.138) | copy-start | bytes 24580
  71.3 377.9 %copy-start.14 = (f32[2048]{0:T(1024)}, f32[2048]{0:T(1024)S(1)}, u32[]{:S(2)}) copy-start(f32[2048]{0:T(1024)S(1)} %get-tuple-element.141) | copy-start | bytes 24580
  71.3 384.2 %copy-start.16 = (f32[2048]{0:T(1024)}, f32[2048]{0:T(1024)S(1)}, u32[]{:S(2)}) copy-start(f32[2048]{0:T(1024)S(1)} %get-tuple-element.140) | copy-start | bytes 24580
  71.3 389.7 %copy-start.18 = (f32[2048]{0:T(1024)}, f32[2048]{0:T(1024)S(1)}, u32[]{:S(2)}) copy-start(f32[2048]{0:T(1024)S(1)} %get-tuple-element.132) | copy-start | bytes 24580
  71.4 392.9 %copy-start.20 = (f32[2048]{0:T(1024)}, f32[2048]{0:T(1024)S(1)}, u32[]{:S(2)}) copy-start(f32[2048]{0:T(1024)S(1)} %get-tuple-element.133) | copy-start | bytes 24580
  443.5 39.1 %copy-start.1 = (f32[256,2048]{1,0:T(8,128)}, f32[256,2048]{1,0:T(8,128)S(1)}, u32[]{:S(2)}) copy-start(f32[256,2048]{1,0:T(8,128)S(1)} %multiply_add_fusion) | copy-start | bytes 6291460
  450.9 28.6 %copy-start.5 = (f32[128,2048]{1,0:T(8,128)}, f32[128,2048]{1,0:T(8,128)S(1)}, u32[]{:S(2)}) copy-start(f32[128,2048]{1,0:T(8,128)S(1)} %multiply_add_fusion.1) | copy-start | bytes 3145732
  468.0 19.3 %slice-start.3 = ((f32[8,2048]{1,0:T(8,128)}), f32[1,2048]{1,0:T(1,128)S(1)}, s32[]{:S(2)}) async-start(f32[8,2048]{1,0:T(8,128)} %multiply_add_fusion.5), calls=%async_computation.5 | async-start | bytes 16384 | tf_op jit(solution)/shard_map/slice | solution.py:56
  477.8 9.8 %copy-start.10 = (f32[15,2048]{1,0:T(8,128)S(1)}, f32[15,2048]{1,0:T(8,128)}, u32[]{:S(2)}) copy-start(f32[15,2048]{1,0:T(8,128)} %slice.246) | copy-start | bytes 368644
  479.5 7.9 %copy-start.11 = (f32[7,2048]{1,0:T(8,128)S(1)}, f32[7,2048]{1,0:T(8,128)}, u32[]{:S(2)}) copy-start(f32[7,2048]{1,0:T(8,128)} %slice.244) | copy-start | bytes 172036
  479.6 7.9 %copy-start.22 = (f32[2048]{0:T(1024)S(1)}, f32[2048]{0:T(1024)}, u32[]{:S(2)}) copy-start(f32[2048]{0:T(1024)} %get-tuple-element.135) | copy-start | bytes 24580
  479.6 7.9 %copy-start.27 = (f32[1,2048]{1,0:T(1,128)S(1)}, f32[1,2048]{1,0:T(1,128)}, u32[]{:S(2)}) copy-start(f32[1,2048]{1,0:T(1,128)} %slice.262) | copy-start | bytes 24580
  479.6 8.0 %copy-start.21 = (f32[2048]{0:T(1024)S(1)}, f32[2048]{0:T(1024)}, u32[]{:S(2)}) copy-start(f32[2048]{0:T(1024)} %copy-done.20) | copy-start | bytes 24580
  479.6 8.0 %copy-start.26 = (f32[1,2048]{1,0:T(1,128)S(1)}, f32[1,2048]{1,0:T(1,128)}, u32[]{:S(2)}) copy-start(f32[1,2048]{1,0:T(1,128)} %slice.261) | copy-start | bytes 24580
  490.2 5.3 copy-start.15
  507.9 16.7 %copy-start.3 = (f32[256,2048]{1,0:T(8,128)S(1)}, f32[256,2048]{1,0:T(8,128)}, u32[]{:S(2)}) copy-start(f32[256,2048]{1,0:T(8,128)} %add.183) | copy-start | bytes 6291460
  524.6 25.5 %copy-start.23 = (f32[2048]{0:T(1024)S(1)}, f32[2048]{0:T(1024)}, u32[]{:S(2)}) copy-start(f32[2048]{0:T(1024)} %get-tuple-element.131) | copy-start | bytes 24580
  524.7 25.5 %copy-start.24 = (f32[2048]{0:T(1024)S(1)}, f32[2048]{0:T(1024)}, u32[]{:S(2)}) copy-start(f32[2048]{0:T(1024)} %get-tuple-element.142) | copy-start | bytes 24580
  524.7 25.5 %copy-start.28 = (f32[512]{0:T(512)S(1)}, f32[512]{0:T(512)}, u32[]{:S(2)}) copy-start(f32[512]{0:T(512)} %iota_add_fusion) | copy-start | bytes 6148
  (14 other events, 22.9 us)
Sparse Core Ops, SparseCore 0:
  70.0 154.7 all-gather.4
  226.6 158.9 all-gather.6
where the time goes:
time: 566 us; the launch traced here: 564 us
  waiting for transfers between devices  300 us (53%)
  local copies, waits for them, and re-layouts  111 us (20%)
  matrix products  71.2 us (13%)
  other arithmetic  40.3 us (7%)
  blocking collectives  23.3 us (4%)
  between operations  14.7 us (3%)
    all_gather x1, waiting for transfers between devices, body(): all_rows = lax.all_gather(mr_out, 'ctx', axis=0, tiled=True)  161 us
    all_gather x1, waiting for transfers between devices, body(): gathered = lax.all_gather(gated, 'mp', axis=1, tiled=True)  138 us
    slice x34, local copies, waits for them, and re-layouts, body(): lax.associative_scan(link_pair, (decay_rows, drive_li), axis=0)  61.5 us
    conv_general_dilated x1, matrix products, body(): lax.conv_general_dilated(padded, kernel, (1,), 'VALID', dimension_numbers...  45.6 us
    pad x16, local copies, waits for them, and re-layouts, body(): lax.associative_scan(link_pair, (decay_rows, drive_li), axis=0)  35.5 us
    dot_general x1, matrix products, body(): summed = jnp.dot(gathered, all_rows, preferred_element_type=jnp.float32)  25.6 us
    all_gather x2, blocking collectives, carried_in(): pieces = jax.tree.map(lambda part: lax.all_gather(part, axis), value)  23.3 us
    add x16, other arithmetic, link_pair(): return (earlier[0] * later[0], later[0] * earlier[1] + later[1])  16.2 us
  transfers between devices with their start and end apart: 3, of which 2 were waited for; matrix products, arithmetic and copies ran while one was open for 1% of the time, Pallas kernels for 0%

commit v1 on v0

--- a/solution.py
+++ b/solution.py
@@ -46,7 +46,14 @@
         precision=lax.Precision.HIGHEST,
     )[0]
     gated = (q_mr.astype(jnp.float32) * filtered).astype(jnp.bfloat16)
-    gathered = lax.all_gather(gated, "mp", axis=1, tiled=True)
+    count_2 = lax.axis_size("mp")
+    right = [(i_2, (i_2 + 1) % count_2) for i_2 in range(count_2)]
+    parts = [gated]
+    for stride in range(1, count_2):
+        parts = [lax.ppermute(parts[0], "mp", right), *parts]
+    whole = jnp.concatenate(parts, axis=1)
+    shift = (lax.axis_index("mp") + 1) * parts[-1].shape[1]
+    gathered = jnp.roll(whole, shift, axis=1)
     all_rows = lax.all_gather(mr_out, "ctx", axis=0, tiled=True)
     summed = jnp.dot(gathered, all_rows, preferred_element_type=jnp.float32)
     mixed = (resid_in.astype(jnp.float32) + summed).astype(jnp.bfloat16)

time: 566 us -> 414 us (0.73)
  waiting for transfers between devices: 300 us -> 136 us
  local copies, waits for them, and re-layouts: 111 us -> 129 us
  blocking collectives: 23.3 us -> 17.2 us
    all_gather x1, waiting for transfers between devices: 161 us -> 0.01 us  [body(): all_rows = lax.all_gather(mr_out, 'ctx', axis=0, tiled=True)]
    all_gather x1 -> x0, waiting for transfers between devices: 138 us -> none  [body(): gathered = lax.all_gather(gated, 'mp', axis=1, tiled=True)]
    ppermute x0 -> x3, waiting for transfers between devices: none -> 136 us  [body(): parts = [lax.ppermute(parts[0], 'mp', right), *parts]]
    unnamed x63 -> x78, local copies, waits for them, and re-layouts: 1.57 us -> 18.8 us
    all_gather x2, blocking collectives: 23.3 us -> 17.2 us  [carried_in(): pieces = jax.tree.map(lambda part: lax.all_gather(part, axis), value)]
  transfers between devices with their start and end apart: 3 -> 5, of which waited for: 2 -> 3; matrix products, arithmetic and copies ran while one was open for 1% -> 19% of each run, Pallas kernels for 0% -> 0%
where the time goes in v1:
time: 414 us; the launch traced here: 412 us
  waiting for transfers between devices  136 us (33%)
  local copies, waits for them, and re-layouts  129 us (31%)
  matrix products  71.3 us (17%)
  other arithmetic  37.2 us (9%)
  blocking collectives  17.2 us (4%)
  between operations  14.8 us (4%)
  starting transfers between devices  5.91 us (1%)
    ppermute x3, waiting for transfers between devices, body(): parts = [lax.ppermute(parts[0], 'mp', right), *parts]  136 us
    slice x34, local copies, waits for them, and re-layouts, body(): lax.associative_scan(link_pair, (decay_rows, drive_li), axis=0)  61 us
    conv_general_dilated x1, matrix products, body(): lax.conv_general_dilated(padded, kernel, (1,), 'VALID', dimension_numbers...  45.6 us
    pad x16, local copies, waits for them, and re-layouts, body(): lax.associative_scan(link_pair, (decay_rows, drive_li), axis=0)  35.2 us
    dot_general x1, matrix products, body(): summed = jnp.dot(gathered, all_rows, preferred_element_type=jnp.float32)  25.7 us
    unnamed x78, local copies, waits for them, and re-layouts  18.8 us
    all_gather x2, blocking collectives, carried_in(): pieces = jax.tree.map(lambda part: lax.all_gather(part, axis), value)  17.2 us
    add x16, other arithmetic, link_pair(): return (earlier[0] * later[0], later[0] * earlier[1] + later[1])  15.7 us
  transfers between devices with their start and end apart: 5, of which 3 were waited for; matrix products, arithmetic and copies ran while one was open for 19% of the time, Pallas kernels for 0%

profile of v1, /device:TPU:0, one launch (start us, length us, event | category | flops | bytes accessed | tf_op | source)
XLA Modules:
  0.0 412.0 jit_solution(18292344556680172116)
XLA Ops:
  11.9 3.2 collective-permute-start
  15.1 5.2 %rev.3 = f32[128,2048]{1,0:T(8,128)} reverse(f32[128,2048]{1,0:T(8,128)S(1)} %copy-done.6), dimensions={0} | reverse | bytes 2097152 | tf_op jit(solution)/shard_map/rev | solution.py:38
  22.2 45.6 %fusion.2 = f32[1,512,2048]{2,0,1:T(1,128)S(1)} fusion(bf16[1,639,2048]{2,1,0:T(8,128)(2,1)S(1)} %maximum_bitcast_fusion, f32[128,1,2048]{2,0,1:T(8,128)S(1)} %bitcast.21), kind=kOutput, calls=%fused_computation.5 | convolution fusion | flops 1610612736 | bytes 7860224 | tf_op jit(solution)/shard_map/conv_general_dilated | solution.py:39
  72.7 47.2 %collective-permute-done.1 = bf16[512,2048]{1,0:T(8,128)(2,1)S(1)} collective-permute-done((bf16[512,2048]{1,0:T(8,128)(2,1)S(1)}, bf16[512,2048]{1,0:T(8,128)(2,1)S(1)}, u32[]{:S(2)}, u32[]{:S(2)}) %collective-permute-start.1) | collective-permute-done | bytes 2097184 | tf_op jit(solution)/shard_map/ppermute | solution.py:53
  121.4 50.0 %collective-permute-done.2 = bf16[512,2048]{1,0:T(8,128)(2,1)} collective-permute-done((bf16[512,2048]{1,0:T(8,128)(2,1)S(1)}, bf16[512,2048]{1,0:T(8,128)(2,1)}, u32[]{:S(2)}, u32[]{:S(2)}) %collective-permute-start.2) | collective-permute-done | bytes 2097184 | tf_op jit(solution)/shard_map/ppermute | solution.py:53
  172.1 9.4 %all-gather = f32[16384]{0:T(1024)S(1)} all-gather(f32[2048]{0:T(1024)S(1)} %get-tuple-element.139), channel_id=2, replica_groups=mesh['ctx'=8,'mp'=4] {'ctx'}, dimensions={0}, use_global_device_ids=true | all-gather | bytes 73728 | tf_op jit(solution)/shard_map/all_gather | solution.py:15
  182.8 38.4 %collective-permute-done.3 = bf16[512,2048]{1,0:T(8,128)(2,1)} collective-permute-done((bf16[512,2048]{1,0:T(8,128)(2,1)}, bf16[512,2048]{1,0:T(8,128)(2,1)}, u32[]{:S(2)}, u32[]{:S(2)}) %collective-permute-start.3) | collective-permute-done | bytes 2097184 | tf_op jit(solution)/shard_map/ppermute | solution.py:53
  221.2 3.1 constant_dynamic-update-slice_fusion.7
  224.3 3.1 constant_dynamic-update-slice_fusion.6
  230.3 3.1 constant_dynamic-update-slice_fusion.3
  233.4 3.1 constant_dynamic-update-slice_fusion.2
  239.3 25.7 %convert_multiply_fusion = (f32[512,2048]{1,0:T(8,128)}, bf16[512,2048]{1,0:T(8,128)(2,1)}) fusion(bf16[512,2048]{1,0:T(8,128)(2,1)} %param.19, bf16[8192,2048]{1,0:T(8,128)(2,1)} %all-gather.4.cloned.1.call-done, bf16[512,16384]{1,0:T(8,128)(2,1)} %constant_dynamic-update-slice_fusion, s32[]{:T(128)S(6)} %select_n.36, bf16[512,2048]{1,0:T(8,128)(2,1)} %param.12), kind=kOutput, calls=%fused_computation.10 | convolution fusion | flops 17186160640 | bytes 52428804 | tf_op jit(solution)/shard_map/dot_general | solution.py:58
  265.0 9.8 %slice.199 = f32[256,2048]{1,0:T(8,128)} slice(f32[512,2048]{1,0:T(8,128)} %get-tuple-element.143), slice={[0:511:2], [0:2048:1]} | slice | bytes 4194304 | tf_op jit(solution)/shard_map/slice | solution.py:63
  274.8 9.8 %slice.200 = f32[256,2048]{1,0:T(8,128)} slice(f32[512,2048]{1,0:T(8,128)} %get-tuple-element.143), slice={[1:512:2], [0:2048:1]} | slice | bytes 4194304 | tf_op jit(solution)/shard_map/slice | solution.py:63
  287.2 3.3 slice.204
  325.9 10.1 %slice.254 = f32[255,2048]{1,0:T(8,128)} slice(f32[512,2048]{1,0:T(8,128)} %get-tuple-element.143), slice={[2:512:2], [0:2048:1]} | slice | bytes 4177920 | tf_op jit(solution)/shard_map/slice | solution.py:63
  342.4 4.2 %pad.69 = f32[256,2048]{1,0:T(8,128)S(1)} pad(f32[128,2048]{1,0:T(8,128)} %pad_maximum_fusion.1, f32[]{:T(128)} %constant.64.clone.1), padding=0_1_1x0_0_0 | pad | bytes 3145732 | tf_op jit(solution)/shard_map/pad | solution.py:63
  346.6 4.8 %pad.70 = f32[256,2048]{1,0:T(8,128)} pad(f32[128,2048]{1,0:T(8,128)S(1)} %add.197, f32[]{:T(128)} %constant.64.clone.1), padding=1_0_1x0_0_0 | pad | bytes 3145732 | tf_op jit(solution)/shard_map/pad | solution.py:63
  351.4 3.2 add.199
  354.6 16.5 %pad.72 = f32[512,2048]{1,0:T(8,128)} pad(f32[256,2048]{1,0:T(8,128)} %add.199, f32[]{:T(128)} %constant.64.clone.1), padding=1_0_1x0_0_0 | pad | bytes 6291460 | tf_op jit(solution)/shard_map/pad | solution.py:63
  374.2 9.0 %pad.71 = f32[512,2048]{1,0:T(8,128)} pad(f32[256,2048]{1,0:T(8,128)S(1)} %pad_maximum_fusion, f32[]{:T(128)} %constant.64.clone.1), padding=0_1_1x0_0_0 | pad | bytes 6291460 | tf_op jit(solution)/shard_map/pad | solution.py:63
  384.1 7.8 %all-gather.1 = f32[8,1,2048]{2,1,0:T(1,128)S(1)} all-gather(f32[1,1,2048]{2,1,0:T(1,128)S(1)} %add_bitcast_fusion), channel_id=1, replica_groups=mesh['ctx'=8,'mp'=4] {'ctx'}, dimensions={0}, use_global_device_ids=true | all-gather | bytes 73728 | tf_op jit(solution)/shard_map/all_gather | solution.py:15
  391.9 6.3 %while.14 = (s32[]{:T(128)}, f32[2048]{0:T(1024)S(1)}, s32[]{:T(128)}, f32[8,2048]{1,0:T(8,128)}, f32[8,2048]{1,0:T(8,128)S(1)}, /*index=5*/s32[]{:T(128)}, s32[]{:T(128)}) while((s32[]{:T(128)}, f32[2048]{0:T(1024)S(1)}, s32[]{:T(128)}, f32[8,2048]{1,0:T(8,128)}, f32[8,2048]{1,0:T(8,128)S(1)}, /*index=5*/s32[]{:T(128)}, ...), condition=%wide.region_1.2_spmd.clone, body=%wide.region_0.1_spmd.clone.sunk | while | flops 8196 | bytes 65637 | solution.py:24
  398.3 6.9 %multiply_convert_fusion = bf16[512,2048]{1,0:T(8,128)(2,1)} fusion(f32[512,2048]{1,0:T(8,128)} %pad.71, f32[512,2048]{1,0:T(8,128)} %pad.72, bf16[512,2048]{1,0:T(8,128)(2,1)} %param.18, f32[2048]{0:T(1024)S(1)} %get-tuple-element.96, f32[512]{0:T(512)S(1)} %copy-done.32, f32[2048]{0:T(1024)S(1)} %copy-done.27, f32[2048]{0:T(1024)S(1)} %copy-done.26), kind=kLoop, calls=%fused_computation.9 | loop fusion | flops 8388608 | bytes 12609536 | tf_op jit(solution)/shard_map/convert_element_type | solution.py:73
  (179 shorter events, 74.5 us)
Async XLA Ops:
  7.2 232.2 %all-gather.4.cloned.1.call-start = ((), (), s32[]{:S(2)}) async-start(), calls=%async_computation | async-start | bytes 37748736 | tf_op jit(solution)/shard_map/all_gather | solution.py:57
  11.9 8.4 %collective-permute-start = (bf16[127,2048]{1,0:T(8,128)(2,1)}, bf16[127,2048]{1,0:T(8,128)(2,1)}, u32[]{:S(2)}, u32[]{:S(2)}) collective-permute-start(bf16[127,2048]{1,0:T(8,128)(2,1)} %slice.256), channel_id=1, source_target_pairs={{0,4},{4,8},{8,12},{12,16},{16,20},{20,24},{24,28},{1,5},{5,9},{9,... | collective-permute-start | bytes 1560584 | tf_op jit(solution)/shard_map/ppermute | solution.py:10
  22.2 45.6 %copy-start.5 = (bf16[512,2048]{1,0:T(8,128)(2,1)S(1)}, bf16[512,2048]{1,0:T(8,128)(2,1)}, u32[]{:S(2)}) copy-start(bf16[512,2048]{1,0:T(8,128)(2,1)} %param.13) | copy-start | bytes 6291460
  67.8 103.6 %copy-start.33 = (f32[2048]{0:T(1024)S(1)}, f32[2048]{0:T(1024)}, u32[]{:S(2)}) copy-start(f32[2048]{0:T(1024)} %param.21) | copy-start | bytes 24580
  67.8 103.6 %copy-start.34 = (f32[2048]{0:T(1024)S(1)}, f32[2048]{0:T(1024)}, u32[]{:S(2)}) copy-start(f32[2048]{0:T(1024)} %param.20) | copy-start | bytes 24580
  70.2 49.7 %collective-permute-start.1 = (bf16[512,2048]{1,0:T(8,128)(2,1)S(1)}, bf16[512,2048]{1,0:T(8,128)(2,1)S(1)}, u32[]{:S(2)}, u32[]{:S(2)}) collective-permute-start(bf16[512,2048]{1,0:T(8,128)(2,1)S(1)} %fusion.4), channel_id=1, source_target_pairs={{0,1},{1,2},{2,3},{3,0},{4,5},{5,6},{6,7},{7,4},{8,9},{9,10},{10,1... | collective-permute-start | bytes 6291464 | tf_op jit(solution)/shard_map/ppermute | solution.py:53
  121.2 50.2 %collective-permute-start.2 = (bf16[512,2048]{1,0:T(8,128)(2,1)S(1)}, bf16[512,2048]{1,0:T(8,128)(2,1)}, u32[]{:S(2)}, u32[]{:S(2)}) collective-permute-start(bf16[512,2048]{1,0:T(8,128)(2,1)S(1)} %collective-permute-done.1), channel_id=1, source_target_pairs={{0,1},{1,2},{2,3},{3,0},{4,5},{5,6},{6,7},{7,4},{8,9},{9,10},{10,1... | collective-permute-start | bytes 6291464 | tf_op jit(solution)/shard_map/ppermute | solution.py:53
  171.4 49.8 %collective-permute-start.3 = (bf16[512,2048]{1,0:T(8,128)(2,1)}, bf16[512,2048]{1,0:T(8,128)(2,1)}, u32[]{:S(2)}, u32[]{:S(2)}) collective-permute-start(bf16[512,2048]{1,0:T(8,128)(2,1)} %collective-permute-done.2), channel_id=1, source_target_pairs={{0,1},{1,2},{2,3},{3,0},{4,5},{5,6},{6,7},{7,4},{8,9},{9,10},{10,1... | collective-permute-start | bytes 6291464 | tf_op jit(solution)/shard_map/ppermute | solution.py:53
  172.1 112.6 %copy-start.11 = (f32[2048]{0:T(1024)}, f32[2048]{0:T(1024)S(1)}, u32[]{:S(2)}) copy-start(f32[2048]{0:T(1024)S(1)} %get-tuple-element.138) | copy-start | bytes 24580
  172.1 121.2 %copy-start.13 = (f32[2048]{0:T(1024)}, f32[2048]{0:T(1024)S(1)}, u32[]{:S(2)}) copy-start(f32[2048]{0:T(1024)S(1)} %get-tuple-element.141) | copy-start | bytes 24580
  172.1 125.9 %copy-start.15 = (f32[2048]{0:T(1024)}, f32[2048]{0:T(1024)S(1)}, u32[]{:S(2)}) copy-start(f32[2048]{0:T(1024)S(1)} %get-tuple-element.140) | copy-start | bytes 24580
  172.1 131.4 %copy-start.17 = (f32[2048]{0:T(1024)}, f32[2048]{0:T(1024)S(1)}, u32[]{:S(2)}) copy-start(f32[2048]{0:T(1024)S(1)} %get-tuple-element.132) | copy-start | bytes 24580
  172.1 133.8 %copy-start.19 = (f32[2048]{0:T(1024)}, f32[2048]{0:T(1024)S(1)}, u32[]{:S(2)}) copy-start(f32[2048]{0:T(1024)S(1)} %get-tuple-element.133) | copy-start | bytes 24580
  182.8 44.7 %copy-start.2 = (bf16[512,2048]{1,0:T(8,128)(2,1)S(1)}, bf16[512,2048]{1,0:T(8,128)(2,1)}, u32[]{:S(2)}) copy-start(bf16[512,2048]{1,0:T(8,128)(2,1)} %copy-done.1) | copy-start | bytes 6291460
  287.2 38.7 %copy-start = (f32[256,2048]{1,0:T(8,128)}, f32[256,2048]{1,0:T(8,128)S(1)}, u32[]{:S(2)}) copy-start(f32[256,2048]{1,0:T(8,128)S(1)} %multiply_add_fusion) | copy-start | bytes 6291460
  295.0 27.8 %copy-start.3 = (f32[128,2048]{1,0:T(8,128)}, f32[128,2048]{1,0:T(8,128)S(1)}, u32[]{:S(2)}) copy-start(f32[128,2048]{1,0:T(8,128)S(1)} %multiply_add_fusion.1) | copy-start | bytes 3145732
  320.1 17.6 %slice-start.3 = ((f32[8,2048]{1,0:T(8,128)}), f32[1,2048]{1,0:T(1,128)S(1)}, s32[]{:S(2)}) async-start(f32[8,2048]{1,0:T(8,128)} %multiply_add_fusion.5), calls=%async_computation.4 | async-start | bytes 16384 | tf_op jit(solution)/shard_map/slice | solution.py:63
  322.9 15.0 %copy-start.8 = (f32[7,2048]{1,0:T(8,128)S(1)}, f32[7,2048]{1,0:T(8,128)}, u32[]{:S(2)}) copy-start(f32[7,2048]{1,0:T(8,128)} %slice.244) | copy-start | bytes 172036
  322.9 15.0 %copy-start.31 = (f32[1,2048]{1,0:T(1,128)S(1)}, f32[1,2048]{1,0:T(1,128)}, u32[]{:S(2)}) copy-start(f32[1,2048]{1,0:T(1,128)} %slice.262) | copy-start | bytes 24580
  322.9 15.1 %copy-start.20 = (f32[2048]{0:T(1024)S(1)}, f32[2048]{0:T(1024)}, u32[]{:S(2)}) copy-start(f32[2048]{0:T(1024)} %copy-done.19) | copy-start | bytes 24580
  354.6 16.5 %copy-start.12 = (f32[2048]{0:T(1024)S(1)}, f32[2048]{0:T(1024)}, u32[]{:S(2)}) copy-start(f32[2048]{0:T(1024)} %copy-done.11) | copy-start | bytes 24580
  374.2 24.0 %copy-start.26 = (f32[2048]{0:T(1024)S(1)}, f32[2048]{0:T(1024)}, u32[]{:S(2)}) copy-start(f32[2048]{0:T(1024)} %get-tuple-element.131) | copy-start | bytes 24580
  374.2 24.0 %copy-start.27 = (f32[2048]{0:T(1024)S(1)}, f32[2048]{0:T(1024)}, u32[]{:S(2)}) copy-start(f32[2048]{0:T(1024)} %get-tuple-element.142) | copy-start | bytes 24580
  374.2 24.0 %copy-start.32 = (f32[512]{0:T(512)S(1)}, f32[512]{0:T(512)}, u32[]{:S(2)}) copy-start(f32[512]{0:T(512)} %iota_add_fusion) | copy-start | bytes 6148
  (20 other events, 173.6 us)
Sparse Core Ops, SparseCore 0:
  9.9 163.4 all-gather.3
